TPU v7x, 32 devices: a whole 2x2x4 slice. The times are simulated.
32 devices in a mesh: groups: 2 (over y), ctx: 4 (over z), tm: 2 (over x), tp: 2 (over core).
Axes of the slice: x: 2, y: 2, z: 4, core: 2. Of those that a mesh axis runs over, the one named last changes fastest.
Arguments:
- tokens: bfloat16 [256, 8, 1024], P(('groups', 'tm'), 'ctx'), parts along dimension 0, may hold values from -6 to 6
- norm_gain: float32 [1024], replicated, may hold values from 0.1 to 1.9
- block_mask: int32 [4, 4, 4], P(('groups', 'tm'), 'ctx'), parts along dimension 0, may hold values from 0 to 1, as said below
- w_query: bfloat16 [1024, 1024], P('tm', 'tp'), may hold values from -1.25 to 1.25
- w_key: bfloat16 [1024, 1024], P('tm', 'tp'), may hold values from -1.25 to 1.25
- w_value: bfloat16 [1024, 1024], P('tm', 'tp'), may hold values from -0.1875 to 0.1875
- w_out: bfloat16 [1024, 1024], P('tp', 'tm'), may hold values from -0.1875 to 0.1875
- w_up: bfloat16 [1024, 2048], P('tm', 'tp'), may hold values from -0.1875 to 0.1875
- w_down: bfloat16 [2048, 1024], P('tp', 'tm'), may hold values from -0.125 to 0.125
- conv_weight: float32 [5, 1024], P(None, 'tp'), may hold values from -2.5 to 2.5
Outputs:
- denoised: bfloat16 [256, 8, 1024], P(('groups', 'tm'), 'ctx', 'tp'), parts along dimension 0
There are 2 independent parts, one for each index of `groups`. A program takes and returns all parts, laid end to end along the dimension named above; an argument that names none is the same for every part. Nothing has to cross between parts.
Inputs may be any that keep to these rules, and one draw needn't show every extreme that they name: block_mask[w, i, i] is 1 for every window w and block i.
All inputs are finite; a program needn't handle non-finite values.
Results may differ from a plain program's by a relative error of at most 0.0076.
Values may be sent and summed in bfloat16 or wider, within the bound.
A program may use at most 64 MiB of HBM per device.

v0:
```python
import jax
import jax.numpy as jnp
from jax import lax
from jax.sharding import PartitionSpec as P

HEAD_DIM = 64
KERNEL = 5


def from_behind(value, axis, steps):
    count = lax.axis_size(axis)
    first, last = (max(0, -steps), min(count, count - steps))
    return lax.ppermute(value, axis, [(source, source + steps) for source in range(first, last)])


def rms_norm(tokens, norm_gain):
    values = tokens.astype(jnp.float32)
    square = jnp.mean(values * values, axis=-1, keepdims=True)
    return (values * lax.rsqrt(square + 1e-05) * norm_gain).astype(jnp.bfloat16)


def on_device(
    tokens, norm_gain, block_mask, w_query, w_key, w_value, w_out, w_up, w_down, conv_weight
):
    frames_here, dancers_here, width = tokens.shape
    rows_here = frames_here * dancers_here
    normed_grid = rms_norm(tokens, norm_gain)
    normed = normed_grid.reshape(rows_here, width)
    pieces = (
        lax.all_gather(w_query, "tm", axis=0, tiled=True),
        lax.all_gather(w_key, "tm", axis=0, tiled=True),
        lax.all_gather(w_value, "tm", axis=0, tiled=True),
        lax.all_gather(w_up, "tm", axis=0, tiled=True),
    )
    query_sum, key_sum, value_sum, hidden = tuple(
        (jnp.dot(normed, piece_one, preferred_element_type=jnp.float32) for piece_one in pieces)
    )
    local_heads = query_sum.shape[1] // HEAD_DIM
    queries = query_sum.astype(jnp.bfloat16).reshape(rows_here, local_heads, HEAD_DIM)
    key_grid = key_sum.astype(jnp.bfloat16).reshape(
        frames_here, dancers_here, local_heads * HEAD_DIM
    )
    value_grid = value_sum.astype(jnp.bfloat16).reshape(
        frames_here, dancers_here, local_heads * HEAD_DIM
    )
    mask_row = block_mask[0, 0].astype(jnp.float32)
    cycle_blocks = mask_row.shape[0]
    key_piece = lax.all_gather(key_grid, "ctx", axis=1, tiled=True)
    value_piece = lax.all_gather(value_grid, "ctx", axis=1, tiled=True)
    count = key_piece.shape[1]
    block_ids = jnp.arange(count) // dancers_here
    picker = (block_ids[:, None] == jnp.arange(cycle_blocks)[None, :]).astype(jnp.float32)
    allowed_dancers = jnp.dot(picker, mask_row)
    peak_old = jnp.full((local_heads, rows_here), -1e30, jnp.float32)
    key_rows = key_piece.reshape(frames_here * count, local_heads, HEAD_DIM)
    value_rows = value_piece.reshape(frames_here * count, local_heads, HEAD_DIM)
    allowed = jnp.tile(allowed_dancers, frames_here)
    scores = (
        jnp.einsum("qhd,khd->hqk", queries, key_rows, preferred_element_type=jnp.float32) * 0.125
    )
    scores = jnp.where(allowed[None, None, :] > 0, scores, -1e30)
    peak_new = jnp.maximum(peak_old, jnp.max(scores, axis=-1))
    expo = jnp.exp(scores - peak_new[:, :, None]) * allowed[None, None, :]
    total_new = jnp.sum(expo, axis=-1)
    probs = expo.astype(jnp.bfloat16)
    mixed_new = jnp.einsum("hqk,khd->hqd", probs, value_rows, preferred_element_type=jnp.float32)
    attended = (
        (mixed_new / total_new[:, :, None])
        .transpose(1, 0, 2)
        .reshape(rows_here, local_heads * HEAD_DIM)
        .astype(jnp.bfloat16)
    )
    activated = jax.nn.gelu(hidden, approximate=True).astype(jnp.bfloat16)
    out_full, down_full = (
        lax.all_gather(w_out, "tm", axis=1, tiled=True),
        lax.all_gather(w_down, "tm", axis=1, tiled=True),
    )
    branches = jnp.dot(attended, out_full, preferred_element_type=jnp.float32)
    branches = branches + jnp.dot(activated, down_full, preferred_element_type=jnp.float32)
    mine = lax.psum_scatter(
        branches.astype(jnp.bfloat16), "tp", scatter_dimension=1, tiled=True
    ).astype(jnp.float32)
    features_here = mine.shape[1]
    first_feature = lax.axis_index("tp") * features_here
    normed_cols = lax.dynamic_slice_in_dim(normed_grid, first_feature, features_here, 2)
    padded = jnp.pad(normed_cols.astype(jnp.float32), ((4, 4), (0, 0), (0, 0)))
    extended = jnp.zeros((frames_here + 4, dancers_here, features_here), jnp.float32)
    for offset in range(KERNEL):
        extended = extended + conv_weight[offset] * padded[offset : offset + frames_here + 4]
    convolved = extended[2 : frames_here + 2]
    from_before = from_behind(extended[frames_here + 2 :], "tm", 1)
    from_after = from_behind(extended[0:2], "tm", -1)
    convolved = convolved.at[0:2].add(from_before)
    convolved = convolved.at[frames_here - 2 :].add(from_after)
    token_cols = lax.dynamic_slice_in_dim(tokens, first_feature, features_here, 2).astype(
        jnp.float32
    )
    result = token_cols + mine.reshape(frames_here, dancers_here, features_here) + convolved
    return result.astype(jnp.bfloat16)


def solution(mesh):
    placed = (
        P(("groups", "tm"), "ctx", None),
        P(),
        P(("groups", "tm"), "ctx", None),
        P("tm", "tp"),
        P("tm", "tp"),
        P("tm", "tp"),
        P("tp", "tm"),
        P("tm", "tp"),
        P("tp", "tm"),
        P(None, "tp"),
    )
    return jax.shard_map(
        on_device,
        mesh=mesh,
        in_specs=placed,
        out_specs=P(("groups", "tm"), "ctx", "tp"),
        check_vma=False,
    )
```

profile of v0, /device:TPU:0, one launch (start us, length us, event | category | flops | bytes accessed | tf_op | source)
XLA Modules:
  0.0 189.4 jit_solution(12623946930418223822)
XLA Ops:
  6.5 0.7 all-gather.7.cloned.1.call-update
  7.3 0.7 all-gather.9.cloned.1.call-update
  8.1 0.7 all-gather.11.cloned.1.call-update
  12.0 1.0 fusion.26
  13.0 19.9 %all-gather.7.cloned.1.call-done = bf16[1024,512]{1,0:T(8,128)(2,1)} async-done(((bf16[512,512]{1,0:T(8,128)(2,1)}), bf16[1024,512]{1,0:T(8,128)(2,1)}) %all-gather.7.cloned.1.call-update) | async-done | bytes 1048592 | tf_op jit(solution)/shard_map/all_gather | solution.py:30
  32.9 1.5 convolution_convert_fusion.2
  34.6 21.2 %all-gather.9.cloned.1.call-done = bf16[1024,512]{1,0:T(8,128)(2,1)} async-done(((bf16[512,512]{1,0:T(8,128)(2,1)}), bf16[1024,512]{1,0:T(8,128)(2,1)}) %all-gather.9.cloned.1.call-update) | async-done | bytes 1048592 | tf_op jit(solution)/shard_map/all_gather | solution.py:31
  55.8 1.5 convolution_convert_fusion.1
  57.4 15.5 %all_gather.26 = bf16[64,8,512]{2,0,1:T(8,128)(2,1)S(1)} all-gather(bf16[64,2,512]{2,0,1:T(8,128)(2,1)S(1)} %copy.35), channel_id=1, replica_groups=mesh['groups'=2,'ctx'=4,'tm'=2,'tp'=2] {'ctx'}, dimensions={1}, use_global_device_ids=true | all-gather | bytes 655360 | tf_op jit(solution)/shard_map/all_gather | solution.py:48
  73.7 5.0 %all-gather.11.cloned.1.call-done = bf16[1024,512]{1,0:T(8,128)(2,1)} async-done(((bf16[512,512]{1,0:T(8,128)(2,1)}), bf16[1024,512]{1,0:T(8,128)(2,1)}) %all-gather.11.cloned.1.call-update) | async-done | bytes 1048592 | tf_op jit(solution)/shard_map/all_gather | solution.py:32
  78.6 1.5 convolution_convert_fusion
  80.9 15.5 %all_gather.28 = bf16[64,8,512]{2,0,1:T(8,128)(2,1)S(1)} all-gather(bf16[64,2,512]{2,0,1:T(8,128)(2,1)S(1)} %copy.38), channel_id=1, replica_groups=mesh['groups'=2,'ctx'=4,'tm'=2,'tp'=2] {'ctx'}, dimensions={1}, use_global_device_ids=true | all-gather | bytes 655360 | tf_op jit(solution)/shard_map/all_gather | solution.py:49
  96.6 1.5 reshape.132
  99.4 0.9 fusion.5
  100.2 12.9 %all-gather.17.cloned.1.call-done = bf16[1024,1024]{1,0:T(8,128)(2,1)} async-done(((bf16[1024,512]{1,0:T(8,128)(2,1)}), bf16[1024,1024]{1,0:T(8,128)(2,1)}) %all-gather.17.cloned.1.call-update) | async-done | bytes 2097168 | tf_op jit(solution)/shard_map/all_gather | solution.py:76
  113.2 34.5 %all-gather.15.cloned.1.call-done = bf16[1024,1024]{1,0:T(8,128)(2,1)} async-done(((bf16[512,1024]{1,0:T(8,128)(2,1)}), bf16[1024,1024]{1,0:T(8,128)(2,1)}) %all-gather.15.cloned.1.call-update) | async-done | bytes 2097168 | tf_op jit(solution)/shard_map/all_gather | solution.py:33
  147.7 3.1 %fusion.30 = f32[128,1024]{1,0:T(8,128)S(1)} fusion(bf16[1024,1024]{1,0:T(8,128)(2,1)} %all-gather.17.cloned.1.call-done, bf16[128,1024]{1,0:T(8,128)(2,1)S(1)} %reshape.127, bf16[1024,1024]{1,0:T(8,128)(2,1)} %all-gather.15.cloned.1.call-done), kind=kOutput, calls=%fused_computation.45 | convolution fusion | flops 538050560 | bytes 4980736 | tf_op jit(solution)/shard_map/dot_general | solution.py:79
  150.8 19.6 %all-gather.13.cloned.1.call-done = bf16[512,1024]{1,0:T(8,128)(2,1)} async-done(((bf16[512,512]{1,0:T(8,128)(2,1)}), bf16[512,1024]{1,0:T(8,128)(2,1)}) %all-gather.13.cloned.1.call-update) | async-done | bytes 1048592 | tf_op jit(solution)/shard_map/all_gather | solution.py:75
  170.4 2.3 %fusion.3 = bf16[128,1024]{1,0:T(8,128)(2,1)} fusion(f32[128,1024]{1,0:T(8,128)S(1)} %fusion.30, bf16[128,512]{0,1:T(8,128)(2,1)S(1)} %bitcast.34, bf16[512,1024]{1,0:T(8,128)(2,1)} %all-gather.13.cloned.1.call-done), kind=kOutput, calls=%fused_computation.6 | convolution fusion | flops 134479872 | bytes 1966080 | tf_op jit(solution)/shard_map/dot_general | solution.py:78
  172.7 2.3 %collective-permute-start = (f32[2,2,512]{2,1,0:T(2,128)S(1)}, f32[2,2,512]{2,1,0:T(2,128)S(1)}, u32[]{:S(2)}, u32[]{:S(2)}) collective-permute-start(f32[2,2,512]{2,1,0:T(2,128)S(1)} %get-tuple-element.30), channel_id=1, source_target_pairs={{0,2},{1,3},{4,6},{5,7},{8,10},{9,11},{12,14},{13,15},{16,18},{17,... | collective-permute-start | bytes 24584 | tf_op jit(solution)/shard_map/ppermute | solution.py:13
  175.0 1.3 collective-permute-start.1
  176.3 4.2 %collective-permute-done.1 = f32[2,2,512]{2,1,0:T(2,128)S(1)} collective-permute-done((f32[2,2,512]{2,1,0:T(2,128)S(1)}, f32[2,2,512]{2,1,0:T(2,128)S(1)}, u32[]{:S(2)}, u32[]{:S(2)}) %collective-permute-start.1) | collective-permute-done | bytes 8224 | tf_op jit(solution)/shard_map/ppermute | solution.py:13
  180.6 1.1 reshape.136
  181.7 0.8 add_convert_fusion
  (55 shorter events, 6.5 us)
Async XLA Ops:
  6.5 4.0 %copy-start = (bf16[64,2,1024]{2,1,0:T(2,128)(2,1)S(1)}, bf16[64,2,1024]{2,1,0:T(2,128)(2,1)}, u32[]{:S(2)}) copy-start(bf16[64,2,1024]{2,1,0:T(2,128)(2,1)} %param.14) | copy-start | bytes 786436
  6.5 26.4 %all-gather.7.cloned.1.call-start = ((), (), s32[]{:S(2)}) async-start(), calls=%async_computation.1 | async-start | bytes 1572864 | tf_op jit(solution)/shard_map/all_gather | solution.py:30
  7.3 3.7 %copy-start.5 = (f32[1024]{0:T(1024)S(1)}, f32[1024]{0:T(1024)}, u32[]{:S(2)}) copy-start(f32[1024]{0:T(1024)} %param.15) | copy-start | bytes 12292
  7.3 48.5 %all-gather.9.cloned.1.call-start = ((), (), s32[]{:S(2)}) async-start(), calls=%async_computation.2 | async-start | bytes 1572864 | tf_op jit(solution)/shard_map/all_gather | solution.py:31
  8.0 70.6 %all-gather.11.cloned.1.call-start = ((), (), s32[]{:S(2)}) async-start(), calls=%async_computation.3 | async-start | bytes 1572864 | tf_op jit(solution)/shard_map/all_gather | solution.py:32
  8.8 104.4 %all-gather.17.cloned.1.call-start = ((), (), s32[]{:S(2)}) async-start(), calls=%async_computation.6 | async-start | bytes 3145728 | tf_op jit(solution)/shard_map/all_gather | solution.py:76
  9.3 2.3 %copy-start.4 = (f32[5,512]{1,0:T(8,128)S(1)}, f32[5,512]{1,0:T(8,128)}, u32[]{:S(2)}) copy-start(f32[5,512]{1,0:T(8,128)} %param.23) | copy-start | bytes 30724
  9.3 2.3 %copy-start.6 = (s32[1,1,4]{2,1,0:T(1,128)S(1)}, s32[1,1,4]{2,1,0:T(1,128)}, u32[]{:S(2)}) copy-start(s32[1,1,4]{2,1,0:T(1,128)} %param.16) | copy-start | bytes 52
  9.3 138.3 %all-gather.15.cloned.1.call-start = ((), (), s32[]{:S(2)}) async-start(), calls=%async_computation.5 | async-start | bytes 3145728 | tf_op jit(solution)/shard_map/all_gather | solution.py:33
  9.9 160.5 %all-gather.13.cloned.1.call-start = ((), (), s32[]{:S(2)}) async-start(), calls=%async_computation.4 | async-start | bytes 1572864 | tf_op jit(solution)/shard_map/all_gather | solution.py:75
  10.5 170.1 %reduce-scatter.2.cloned.1.call-start = ((), (), s32[]{:S(2)}) async-start(), calls=%async_computation.7 | async-start | bytes 393216 | tf_op jit(solution)/shard_map/reduce_scatter | solution.py:80
  98.1 1.2 copy-start.3
  150.7 21.9 %copy-start.2 = (f32[68,2,512]{2,1,0:T(2,128)S(1)}, f32[68,2,512]{2,1,0:T(2,128)}, u32[]{:S(2)}) copy-start(f32[68,2,512]{2,1,0:T(2,128)} %fusion.26) | copy-start | bytes 835588
  150.8 25.5 %slice-start = ((f32[68,2,512]{2,1,0:T(2,128)}), f32[64,2,512]{2,1,0:T(2,128)S(1)}, s32[]{:S(2)}) async-start(f32[68,2,512]{2,1,0:T(2,128)} %fusion.26), calls=%async_computation.8 | async-start | bytes 524288 | tf_op jit(solution)/shard_map/slice | solution.py:90
  150.8 30.9 %copy-start.1 = (bf16[64,2,1024]{2,1,0:T(2,128)(2,1)S(1)}, bf16[64,2,1024]{2,1,0:T(2,128)(2,1)}, u32[]{:S(2)}) copy-start(bf16[64,2,1024]{2,1,0:T(2,128)(2,1)} %param.14) | copy-start | bytes 786436
  172.7 3.6 %collective-permute-start = (f32[2,2,512]{2,1,0:T(2,128)S(1)}, f32[2,2,512]{2,1,0:T(2,128)S(1)}, u32[]{:S(2)}, u32[]{:S(2)}) collective-permute-start(f32[2,2,512]{2,1,0:T(2,128)S(1)} %get-tuple-element.30), channel_id=1, source_target_pairs={{0,2},{1,3},{4,6},{5,7},{8,10},{9,11},{12,14},{13,15},{16,18},{17,... | collective-permute-start | bytes 24584 | tf_op jit(solution)/shard_map/ppermute | solution.py:13
  175.0 5.5 %collective-permute-start.1 = (f32[2,2,512]{2,1,0:T(2,128)S(1)}, f32[2,2,512]{2,1,0:T(2,128)S(1)}, u32[]{:S(2)}, u32[]{:S(2)}) collective-permute-start(f32[2,2,512]{2,1,0:T(2,128)S(1)} %get-tuple-element.29), channel_id=1, source_target_pairs={{2,0},{3,1},{6,4},{7,5},{10,8},{11,9},{14,12},{15,13},{18,16},{19,... | collective-permute-start | bytes 24584 | tf_op jit(solution)/shard_map/ppermute | solution.py:13
Sparse Core Ops, SparseCore 0:
  8.9 23.9 all-gather.6
  34.5 21.2 all-gather.8
  57.3 21.2 all-gather.10
  80.0 33.0 all-gather.16
  114.5 33.0 all-gather.14
  149.1 21.2 all-gather.12
  172.8 7.7 reduce-scatter.1
where the time goes:
time: 190 us; the launch traced here: 189 us
  waiting for transfers between devices  121 us (64%)
  blocking collectives  30.9 us (16%)
  between operations  13.8 us (7%)
  matrix products  11.6 us (6%)
  local copies, waits for them, and re-layouts  4.94 us (3%)
  starting transfers between devices  3.77 us (2%)
  other arithmetic  3.36 us (2%)
    all_gather x1, waiting for transfers between devices, on_device(): lax.all_gather(w_up, 'tm', axis=0, tiled=True)  34.5 us
    all_gather x1, waiting for transfers between devices, on_device(): lax.all_gather(w_key, 'tm', axis=0, tiled=True)  21.2 us
    all_gather x1, waiting for transfers between devices, on_device(): lax.all_gather(w_query, 'tm', axis=0, tiled=True)  19.9 us
    all_gather x1, waiting for transfers between devices, on_device(): lax.all_gather(w_out, 'tm', axis=1, tiled=True)  19.6 us
    all_gather x1, blocking collectives, on_device(): key_piece = lax.all_gather(key_grid, 'ctx', axis=1, tiled=True)  15.5 us
    all_gather x1, blocking collectives, on_device(): value_piece = lax.all_gather(value_grid, 'ctx', axis=1, tiled=True)  15.5 us
    all_gather x1, waiting for transfers between devices, on_device(): lax.all_gather(w_down, 'tm', axis=1, tiled=True)  12.9 us
    all_gather x1, waiting for transfers between devices, on_device(): lax.all_gather(w_value, 'tm', axis=0, tiled=True)  4.95 us
  transfers between devices with their start and end apart: 9, of which 8 were waited for; matrix products, arithmetic and copies ran while one was open for 8% of the time, Pallas kernels for 0%

commit v1 on v0

--- a/solution.py
+++ b/solution.py
@@ -45,8 +45,11 @@
     )
     mask_row = block_mask[0, 0].astype(jnp.float32)
     cycle_blocks = mask_row.shape[0]
-    key_piece = lax.all_gather(key_grid, "ctx", axis=1, tiled=True)
-    value_piece = lax.all_gather(value_grid, "ctx", axis=1, tiled=True)
+    key_piece, value_piece = jnp.split(
+        lax.all_gather(jnp.concatenate([key_grid, value_grid], axis=0), "ctx", axis=1, tiled=True),
+        [key_grid.shape[0]],
+        axis=0,
+    )
     count = key_piece.shape[1]
     block_ids = jnp.arange(count) // dancers_here
     picker = (block_ids[:, None] == jnp.arange(cycle_blocks)[None, :]).astype(jnp.float32)

time: 190 us -> 219 us (1.15)
  waiting for transfers between devices: 121 us -> 179 us
  blocking collectives: 30.9 us -> 0 us
    all_gather x2 -> x0, blocking collectives: 30.9 us -> none  [the longest x1 15.5 us: on_device(): key_piece = lax.all_gather(key_grid, 'ctx', axis=1, tiled=True)]
    all_gather x0 -> x1, waiting for transfers between devices: none -> 26.4 us  [on_device(): lax.all_gather(jnp.concatenate([key_grid, value_grid], axis=0), 'ctx', ax...]
    all_gather x1, waiting for transfers between devices: 12.9 us -> 32.9 us  [on_device(): lax.all_gather(w_down, 'tm', axis=1, tiled=True)]
    all_gather x1, waiting for transfers between devices: 4.95 us -> 22.1 us  [on_device(): lax.all_gather(w_value, 'tm', axis=0, tiled=True)]
    all_gather x1, waiting for transfers between devices: 19.6 us -> 16.1 us  [on_device(): lax.all_gather(w_out, 'tm', axis=1, tiled=True)]
  transfers between devices with their start and end apart: 9 -> 10, of which waited for: 8 -> 9; matrix products, arithmetic and copies ran while one was open for 8% -> 8% of each run, Pallas kernels for 0% -> 0%
where the time goes in v1:
time: 219 us; the launch traced here: 218 us
  waiting for transfers between devices  179 us (82%)
  between operations  13.8 us (6%)
  matrix products  11.6 us (5%)
  local copies, waits for them, and re-layouts  5.68 us (3%)
  other arithmetic  3.96 us (2%)
  starting transfers between devices  3.82 us (2%)
    all_gather x1, waiting for transfers between devices, on_device(): lax.all_gather(w_up, 'tm', axis=0, tiled=True)  34.5 us
    all_gather x1, waiting for transfers between devices, on_device(): lax.all_gather(w_down, 'tm', axis=1, tiled=True)  32.9 us
    all_gather x1, waiting for transfers between devices, on_device(): lax.all_gather(jnp.concatenate([key_grid, value_grid], axis=0), 'ctx', ax...  26.4 us
    all_gather x1, waiting for transfers between devices, on_device(): lax.all_gather(w_value, 'tm', axis=0, tiled=True)  22.1 us
    all_gather x1, waiting for transfers between devices, on_device(): lax.all_gather(w_key, 'tm', axis=0, tiled=True)  21.2 us
    all_gather x1, waiting for transfers between devices, on_device(): lax.all_gather(w_query, 'tm', axis=0, tiled=True)  18.2 us
    all_gather x1, waiting for transfers between devices, on_device(): lax.all_gather(w_out, 'tm', axis=1, tiled=True)  16.1 us
    dot_general x3, matrix products, on_device(): jnp.dot(normed, piece_one, preferred_element_type=jnp.float32)  4.59 us
  transfers between devices with their start and end apart: 10, of which 9 were waited for; matrix products, arithmetic and copies ran while one was open for 8% of the time, Pallas kernels for 0%

profile of v1, /device:TPU:0, one launch (start us, length us, event | category | flops | bytes accessed | tf_op | source)
XLA Modules:
  0.0 218.3 jit_solution(15491028782349576179)
XLA Ops:
  6.5 0.7 all-gather.12.cloned.1.call-update
  7.3 0.7 all-gather.10.cloned.1.call-update
  10.8 22.1 %all-gather.12.cloned.1.call-done = bf16[1024,512]{1,0:T(8,128)(2,1)} async-done(((bf16[512,512]{1,0:T(8,128)(2,1)}), bf16[1024,512]{1,0:T(8,128)(2,1)}) %all-gather.12.cloned.1.call-update) | async-done | bytes 1048592 | tf_op jit(solution)/shard_map/all_gather | solution.py:32
  32.9 1.5 convolution_convert_fusion
  34.6 21.2 %all-gather.10.cloned.1.call-done = bf16[1024,512]{1,0:T(8,128)(2,1)} async-done(((bf16[512,512]{1,0:T(8,128)(2,1)}), bf16[1024,512]{1,0:T(8,128)(2,1)}) %all-gather.10.cloned.1.call-update) | async-done | bytes 1048592 | tf_op jit(solution)/shard_map/all_gather | solution.py:31
  55.8 1.5 convolution_convert_fusion.1
  57.4 0.7 pad_maximum_fusion
  58.2 0.7 all-gather.16.cloned.1.call-update
  60.4 18.2 %all-gather.8.cloned.1.call-done = bf16[1024,512]{1,0:T(8,128)(2,1)} async-done(((bf16[512,512]{1,0:T(8,128)(2,1)}), bf16[1024,512]{1,0:T(8,128)(2,1)}) %all-gather.8.cloned.1.call-update) | async-done | bytes 1048592 | tf_op jit(solution)/shard_map/all_gather | solution.py:30
  78.6 1.5 convolution_convert_fusion.2
  80.3 32.9 %all-gather.20.cloned.1.call-done = bf16[1024,1024]{1,0:T(8,128)(2,1)} async-done(((bf16[1024,512]{1,0:T(8,128)(2,1)}), bf16[1024,1024]{1,0:T(8,128)(2,1)}) %all-gather.20.cloned.1.call-update) | async-done | bytes 2097168 | tf_op jit(solution)/shard_map/all_gather | solution.py:79
  113.2 34.5 %all-gather.18.cloned.1.call-done = bf16[1024,1024]{1,0:T(8,128)(2,1)} async-done(((bf16[512,1024]{1,0:T(8,128)(2,1)}), bf16[1024,1024]{1,0:T(8,128)(2,1)}) %all-gather.18.cloned.1.call-update) | async-done | bytes 2097168 | tf_op jit(solution)/shard_map/all_gather | solution.py:33
  147.7 3.1 %fusion.30 = f32[128,1024]{1,0:T(8,128)S(1)} fusion(bf16[1024,1024]{1,0:T(8,128)(2,1)} %all-gather.20.cloned.1.call-done, bf16[128,1024]{1,0:T(8,128)(2,1)S(1)} %reshape.127, bf16[1024,1024]{1,0:T(8,128)(2,1)} %all-gather.18.cloned.1.call-done), kind=kOutput, calls=%fused_computation.45 | convolution fusion | flops 538050560 | bytes 4980736 | tf_op jit(solution)/shard_map/dot_general | solution.py:82
  150.7 26.4 %all-gather.14.cloned.1.call-done = bf16[128,8,512]{2,0,1:T(8,128)(2,1)} async-done(((bf16[128,2,512]{2,0,1:T(8,128)(2,1)}), bf16[128,8,512]{2,0,1:T(8,128)(2,1)}) %all-gather.14.cloned.1.call-update) | async-done | bytes 1048592 | tf_op jit(solution)/shard_map/all_gather | solution.py:49
  177.1 1.3 fusion.45
  179.6 1.6 reshape.132
  182.4 0.9 fusion.5
  183.3 16.1 %all-gather.16.cloned.1.call-done = bf16[512,1024]{1,0:T(8,128)(2,1)} async-done(((bf16[512,512]{1,0:T(8,128)(2,1)}), bf16[512,1024]{1,0:T(8,128)(2,1)}) %all-gather.16.cloned.1.call-update) | async-done | bytes 1048592 | tf_op jit(solution)/shard_map/all_gather | solution.py:78
  199.3 2.3 %fusion.3 = bf16[128,1024]{1,0:T(8,128)(2,1)} fusion(f32[128,1024]{1,0:T(8,128)S(1)} %fusion.30, bf16[128,512]{0,1:T(8,128)(2,1)S(1)} %bitcast.34, bf16[512,1024]{1,0:T(8,128)(2,1)} %all-gather.16.cloned.1.call-done), kind=kOutput, calls=%fused_computation.6 | convolution fusion | flops 134479872 | bytes 1966080 | tf_op jit(solution)/shard_map/dot_general | solution.py:81
  201.6 2.3 %collective-permute-start = (f32[2,2,512]{2,1,0:T(2,128)S(1)}, f32[2,2,512]{2,1,0:T(2,128)S(1)}, u32[]{:S(2)}, u32[]{:S(2)}) collective-permute-start(f32[2,2,512]{2,1,0:T(2,128)S(1)} %get-tuple-element.32), channel_id=1, source_target_pairs={{0,2},{1,3},{4,6},{5,7},{8,10},{9,11},{12,14},{13,15},{16,18},{17,... | collective-permute-start | bytes 24584 | tf_op jit(solution)/shard_map/ppermute | solution.py:13
  203.9 1.3 collective-permute-start.1
  205.3 4.2 %collective-permute-done.1 = f32[2,2,512]{2,1,0:T(2,128)S(1)} collective-permute-done((f32[2,2,512]{2,1,0:T(2,128)S(1)}, f32[2,2,512]{2,1,0:T(2,128)S(1)}, u32[]{:S(2)}, u32[]{:S(2)}) %collective-permute-start.1) | collective-permute-done | bytes 8224 | tf_op jit(solution)/shard_map/ppermute | solution.py:13
  209.5 1.1 reshape.136
  210.6 0.8 add_convert_fusion
  (59 shorter events, 7.1 us)
Async XLA Ops:
  6.5 3.4 %copy-start = (bf16[64,2,1024]{2,1,0:T(2,128)(2,1)S(1)}, bf16[64,2,1024]{2,1,0:T(2,128)(2,1)}, u32[]{:S(2)}) copy-start(bf16[64,2,1024]{2,1,0:T(2,128)(2,1)} %param.14) | copy-start | bytes 786436
  6.5 3.8 %copy-start.6 = (f32[1024]{0:T(1024)S(1)}, f32[1024]{0:T(1024)}, u32[]{:S(2)}) copy-start(f32[1024]{0:T(1024)} %param.15) | copy-start | bytes 12292
  6.5 26.4 %all-gather.12.cloned.1.call-start = ((), (), s32[]{:S(2)}) async-start(), calls=%async_computation.3 | async-start | bytes 1572864 | tf_op jit(solution)/shard_map/all_gather | solution.py:32
  7.3 48.5 %all-gather.10.cloned.1.call-start = ((), (), s32[]{:S(2)}) async-start(), calls=%async_computation.2 | async-start | bytes 1572864 | tf_op jit(solution)/shard_map/all_gather | solution.py:31
  8.0 70.6 %all-gather.8.cloned.1.call-start = ((), (), s32[]{:S(2)}) async-start(), calls=%async_computation.1 | async-start | bytes 1572864 | tf_op jit(solution)/shard_map/all_gather | solution.py:30
  8.7 104.4 %all-gather.20.cloned.1.call-start = ((), (), s32[]{:S(2)}) async-start(), calls=%async_computation.7 | async-start | bytes 3145728 | tf_op jit(solution)/shard_map/all_gather | solution.py:79
  9.3 138.4 %all-gather.18.cloned.1.call-start = ((), (), s32[]{:S(2)}) async-start(), calls=%async_computation.6 | async-start | bytes 3145728 | tf_op jit(solution)/shard_map/all_gather | solution.py:33
  9.9 167.2 %all-gather.14.cloned.1.call-start = ((), (), s32[]{:S(2)}) async-start(), calls=%async_computation.4 | async-start | bytes 1310720 | tf_op jit(solution)/shard_map/all_gather | solution.py:49
  34.5 24.7 %copy-start.4 = (f32[5,512]{1,0:T(8,128)S(1)}, f32[5,512]{1,0:T(8,128)}, u32[]{:S(2)}) copy-start(f32[5,512]{1,0:T(8,128)} %param.23) | copy-start | bytes 30724
  34.5 24.7 %copy-start.7 = (s32[1,1,4]{2,1,0:T(1,128)S(1)}, s32[1,1,4]{2,1,0:T(1,128)}, u32[]{:S(2)}) copy-start(s32[1,1,4]{2,1,0:T(1,128)} %param.16) | copy-start | bytes 52
  58.1 141.2 %all-gather.16.cloned.1.call-start = ((), (), s32[]{:S(2)}) async-start(), calls=%async_computation.5 | async-start | bytes 1572864 | tf_op jit(solution)/shard_map/all_gather | solution.py:78
  58.9 150.6 %reduce-scatter.2.cloned.1.call-start = ((), (), s32[]{:S(2)}) async-start(), calls=%async_computation.8 | async-start | bytes 393216 | tf_op jit(solution)/shard_map/reduce_scatter | solution.py:83
  59.5 0.6 copy-start.2
  178.7 2.4 %copy-start.5 = (pred[512]{0:T(512)(128)(4,1)S(1)}, pred[512]{0:T(512)(128)(4,1)}, u32[]{:S(2)}) copy-start(pred[512]{0:T(512)(128)(4,1)} %broadcast_compare_fusion) | copy-start | bytes 1540
  179.6 2.2 %copy-start.3 = (f32[512]{0:T(512)S(1)}, f32[512]{0:T(512)}, u32[]{:S(2)}) copy-start(f32[512]{0:T(512)} %copy-done.2) | copy-start | bytes 6148
  181.1 1.3 copy-start.1
  201.6 3.6 %collective-permute-start = (f32[2,2,512]{2,1,0:T(2,128)S(1)}, f32[2,2,512]{2,1,0:T(2,128)S(1)}, u32[]{:S(2)}, u32[]{:S(2)}) collective-permute-start(f32[2,2,512]{2,1,0:T(2,128)S(1)} %get-tuple-element.32), channel_id=1, source_target_pairs={{0,2},{1,3},{4,6},{5,7},{8,10},{9,11},{12,14},{13,15},{16,18},{17,... | collective-permute-start | bytes 24584 | tf_op jit(solution)/shard_map/ppermute | solution.py:13
  203.9 5.5 %collective-permute-start.1 = (f32[2,2,512]{2,1,0:T(2,128)S(1)}, f32[2,2,512]{2,1,0:T(2,128)S(1)}, u32[]{:S(2)}, u32[]{:S(2)}) collective-permute-start(f32[2,2,512]{2,1,0:T(2,128)S(1)} %get-tuple-element.31), channel_id=1, source_target_pairs={{2,0},{3,1},{6,4},{7,5},{10,8},{11,9},{14,12},{15,13},{18,16},{19,... | collective-permute-start | bytes 24584 | tf_op jit(solution)/shard_map/ppermute | solution.py:13
Sparse Core Ops, SparseCore 0:
  8.9 23.9 all-gather.11
  34.5 21.2 all-gather.9
  57.3 21.2 all-gather.7
  80.0 33.0 all-gather.19
  114.5 33.0 all-gather.17
  149.1 27.9 all-gather.13
  178.7 20.6 all-gather.15
  201.8 7.7 reduce-scatter.1
